TPU v7x, 256 devices: a whole 4x4x8 slice. The times are simulated.
256 devices in a mesh: gal: 8 (over y, core), pix: 32 (over x, z).
Axes of the slice: x: 4, y: 4, z: 8, core: 2. Of those that a mesh axis runs over, the one named last changes fastest.
Arguments:
- observed: float32 [32768, 4096], P('pix', 'gal'), may hold values from -6 to 6
- sparse_init: float32 [32768, 4096], P('pix', 'gal'), may hold values from -4 to 4
- dual_init: float32 [32768, 4096], P('pix', 'gal'), may hold values from -4 to 4
- right_init: float32 [64, 4096], P(None, 'gal'), may hold values from -0.09375 to 0.09375
Outputs:
- sparse: float32 [32768, 4096], P('pix', 'gal')
- dual: float32 [32768, 4096], P('pix', 'gal')
- left: float32 [64, 32768], P(None, 'pix')
- right: float32 [64, 4096], P(None, 'gal')
All inputs are finite; a program needn't handle non-finite values.
Results may differ from a plain program's by a relative error of at most 0.0003.
Values sent between devices are 32-bit elements; how exact they have to be, the bound alone decides.
A program may use at most 64 MiB of HBM per device.

v0:
```python
import jax
import jax.numpy as jnp
from jax import lax
from jax.sharding import PartitionSpec as P

ITERS = 2
MU = 1.25
TAU = 0.6 / 1.25
HIGH = lax.Precision.HIGHEST


def gram_of(panel):
    return lax.dot_general(panel, panel, (((1,), (1,)), ((), ())), precision=HIGH)


def orth_with(panel, gram):
    factor = jnp.linalg.cholesky(gram)
    return jax.scipy.linalg.solve_triangular(factor, panel, lower=True)


def shrink(values):
    return jnp.sign(values) * jnp.maximum(jnp.abs(values) - TAU, 0.0)


def per_device(observed, sparse_init, dual_init, right_init):
    sparse, dual, right = (sparse_init, dual_init, right_init)
    left = None
    for step in range(ITERS):
        target = observed - sparse + dual / MU
        partial_left = lax.dot_general(right, target, (((1,), (1,)), ((), ())), precision=HIGH)
        panel = lax.psum(partial_left, "gal")
        gram_left = lax.psum(gram_of(panel), "pix")
        left = orth_with(panel, gram_left)
        partial_wide = jnp.dot(left, target, precision=HIGH)
        wide = lax.psum(partial_wide, "pix")
        lowrank = lax.dot_general(left, wide, (((0,), (0,)), ((), ())), precision=HIGH)
        sparse = shrink(observed - lowrank + dual / MU)
        dual = dual + MU * (observed - lowrank - sparse)
        gram_right = lax.psum(gram_of(wide), "gal")
        right = orth_with(wide, gram_right)
    return (sparse, dual, left, right)


def solution(mesh):
    return jax.shard_map(
        per_device,
        mesh=mesh,
        in_specs=(P("pix", "gal"), P("pix", "gal"), P("pix", "gal"), P(None, "gal")),
        out_specs=(P("pix", "gal"), P("pix", "gal"), P(None, "pix"), P(None, "gal")),
        check_vma=False,
    )
```

profile of v0, /device:TPU:2, one launch (start us, length us, event | category | flops | bytes accessed | tf_op | source)
XLA Modules:
  0.0 836.8 jit_solution(9455242366928281128)
XLA Ops:
  7.2 0.0 all-reduce.5.cloned.1.call-start
  7.2 0.8 copy-done
  8.1 6.0 convolution_bitcast_fusion
  14.1 0.0 all-reduce.7.cloned.1.call-start
  14.2 68.6 %all-reduce.5.cloned.1.call-done = f32[64,1024]{1,0:T(8,128)} async-done(((f32[64,1024]{1,0:T(8,128)}), f32[64,1024]{1,0:T(8,128)}) %all-reduce.5.cloned.1.call-update) | async-done | bytes 262160 | tf_op jit(solution)/shard_map/psum | solution.py:31
  82.7 1.4 fusion.21
  84.1 131.0 %psum.57 = f32[64,64]{0,1:T(8,128)S(1)} all-reduce(f32[64,64]{0,1:T(8,128)S(1)} %fusion.21), channel_id=1, replica_groups=mesh['gal'=8,'pix'=32] {'pix'}, use_global_device_ids=true, to_apply=%region_1.0 | all-reduce | flops 4096 | bytes 32768 | tf_op jit(solution)/shard_map/psum | solution.py:32
  215.2 0.1 copy.9
  215.3 5.8 cholesky.74
  221.2 0.6 compare_reduce_fusion.3
  221.8 0.7 fusion
  222.5 4.9 custom-call.10
  227.4 1.4 fusion.13
  228.7 4.4 fusion.20
  233.2 0.0 all-reduce.9.cloned.1.call-start
  233.3 145.8 %all-reduce.7.cloned.1.call-done = f32[64,512]{1,0:T(8,128)} async-done(((f32[64,512]{1,0:T(8,128)}), f32[64,512]{1,0:T(8,128)}) %all-reduce.7.cloned.1.call-update) | async-done | bytes 131088 | tf_op jit(solution)/shard_map/psum | solution.py:35
  379.0 1.2 fusion.22
  380.3 23.8 %psum.59 = f32[64,64]{0,1:T(8,128)S(1)} all-reduce(f32[64,64]{0,1:T(8,128)S(1)} %fusion.22), channel_id=1, replica_groups=mesh['gal'=8,'pix'=32] {'gal'}, use_global_device_ids=true, to_apply=%region_5.8 | all-reduce | flops 4096 | bytes 32768 | tf_op jit(solution)/shard_map/psum | solution.py:39
  404.1 0.1 copy.11
  404.2 5.8 cholesky.85
  410.0 0.6 compare_reduce_fusion.2
  410.7 0.7 fusion.1
  411.4 4.9 custom-call.11
  416.3 6.1 subtract_add_fusion
  422.4 0.3 fusion.10
  422.7 1.0 copy-done.2
  423.7 2.8 fusion.23
  426.6 0.0 all-reduce.11.cloned.1.call-start
  426.6 61.5 %all-reduce.9.cloned.1.call-done = f32[64,1024]{1,0:T(8,128)} async-done(((f32[64,1024]{1,0:T(8,128)}), f32[64,1024]{1,0:T(8,128)}) %all-reduce.9.cloned.1.call-update) | async-done | bytes 262160 | tf_op jit(solution)/shard_map/psum | solution.py:31
  488.1 1.4 fusion.24
  489.5 131.0 %psum.61 = f32[64,64]{0,1:T(8,128)S(1)} all-reduce(f32[64,64]{0,1:T(8,128)S(1)} %fusion.24), channel_id=1, replica_groups=mesh['gal'=8,'pix'=32] {'pix'}, use_global_device_ids=true, to_apply=%region_7.0 | all-reduce | flops 4096 | bytes 32768 | tf_op jit(solution)/shard_map/psum | solution.py:32
  620.6 0.1 copy.13
  620.7 5.8 cholesky.96
  626.5 0.6 compare_reduce_fusion.1
  627.2 0.7 fusion.2
  627.8 4.9 custom-call.12
  632.7 1.4 fusion.7
  634.1 3.7 fusion.25
  637.9 145.9 %all-reduce.11.cloned.1.call-done = f32[64,512]{1,0:T(8,128)} async-done(((f32[64,512]{1,0:T(8,128)}), f32[64,512]{1,0:T(8,128)}) %all-reduce.11.cloned.1.call-update) | async-done | bytes 131088 | tf_op jit(solution)/shard_map/psum | solution.py:35
  783.7 1.2 fusion.26
  785.0 23.8 %psum.63 = f32[64,64]{0,1:T(8,128)S(1)} all-reduce(f32[64,64]{0,1:T(8,128)S(1)} %fusion.26), channel_id=1, replica_groups=mesh['gal'=8,'pix'=32] {'gal'}, use_global_device_ids=true, to_apply=%region_9.13 | all-reduce | flops 4096 | bytes 32768 | tf_op jit(solution)/shard_map/psum | solution.py:39
  808.8 0.1 copy.15
  808.9 5.8 cholesky.107
  814.8 0.6 compare_reduce_fusion
  815.4 0.7 fusion.3
  816.1 4.9 custom-call.13
  821.0 8.2 multiply_add_fusion
  829.3 1.0 fusion.4
  (22 shorter events, 0.3 us)
Async XLA Ops:
  7.2 0.9 copy-start
  7.2 75.6 %all-reduce.5.cloned.1.call-start = ((), (), s32[]{:S(2)}) async-start(), calls=%async_computation | async-start | bytes 524288 | tf_op jit(solution)/shard_map/psum | solution.py:31
  8.1 220.7 %copy-start.1 = (f32[1024,512]{1,0:T(8,128)S(1)}, f32[1024,512]{1,0:T(8,128)}, u32[]{:S(2)}) copy-start(f32[1024,512]{1,0:T(8,128)} %param.11) | copy-start | bytes 6291460
  14.1 364.9 %all-reduce.7.cloned.1.call-start = ((), (), s32[]{:S(2)}) async-start(), calls=%async_computation.1 | async-start | bytes 262144 | tf_op jit(solution)/shard_map/psum | solution.py:35
  233.2 254.9 %all-reduce.9.cloned.1.call-start = ((), (), s32[]{:S(2)}) async-start(), calls=%async_computation.2 | async-start | bytes 524288 | tf_op jit(solution)/shard_map/psum | solution.py:31
  416.2 6.2 copy-start.4
  422.4 1.3 copy-start.2
  426.6 357.1 %all-reduce.11.cloned.1.call-start = ((), (), s32[]{:S(2)}) async-start(), calls=%async_computation.3 | async-start | bytes 262144 | tf_op jit(solution)/shard_map/psum | solution.py:35
  634.1 195.1 %copy-start.3 = (f32[64,1024]{1,0:T(8,128)}, f32[64,1024]{1,0:T(8,128)S(1)}, u32[]{:S(2)}) copy-start(f32[64,1024]{1,0:T(8,128)S(1)} %fusion.7) | copy-start | bytes 786436
  821.0 8.3 copy-start.5
Sparse Core Ops, SparseCore 0:
  14.3 68.4 all-reduce.4
  233.3 145.6 all-reduce.6
  426.7 61.3 all-reduce.8
  638.0 145.6 all-reduce.10
where the time goes:
time: 837 us
  waiting for transfers between devices  422 us (50%)
  blocking collectives  310 us (37%)
  other arithmetic  48.3 us (6%)
  matrix products  40.7 us (5%)
  between operations  14 us (2%)
    psum x2, waiting for transfers between devices, per_device(): wide = lax.psum(partial_wide, 'pix')  292 us
    psum x2, blocking collectives, per_device(): gram_left = lax.psum(gram_of(panel), 'pix')  262 us
    psum x2, waiting for transfers between devices, per_device(): panel = lax.psum(partial_left, 'gal')  130 us
    psum x2, blocking collectives, per_device(): gram_right = lax.psum(gram_of(wide), 'gal')  47.6 us
    another operation x12, other arithmetic, orth_with(): factor = jnp.linalg.cholesky(gram)  26.1 us
    another operation x8, other arithmetic, orth_with(): return jax.scipy.linalg.solve_triangular(factor, panel, lower=True)  22.2 us
  transfers between devices with their start and end apart: 4, of which 4 were waited for; matrix products, arithmetic and copies ran while one was open for 0% of the time, Pallas kernels for 0%

commit v1 on v0

--- a/solution.py
+++ b/solution.py
@@ -7,6 +7,14 @@
 MU = 1.25
 TAU = 0.6 / 1.25
 HIGH = lax.Precision.HIGHEST
+
+
+def add_in_pairs(block, name):
+    n_dev, result = (lax.axis_size(name), block)
+    for hop in [1 << k for k in range(n_dev.bit_length() - 1)]:
+        pairs = [(i, i ^ hop) for i in range(n_dev)]
+        result = result + lax.ppermute(result, name, pairs)
+    return result
 
 
 def gram_of(panel):
@@ -28,7 +36,7 @@
     for step in range(ITERS):
         target = observed - sparse + dual / MU
         partial_left = lax.dot_general(right, target, (((1,), (1,)), ((), ())), precision=HIGH)
-        panel = lax.psum(partial_left, "gal")
+        panel = add_in_pairs(partial_left, "gal")
         gram_left = lax.psum(gram_of(panel), "pix")
         left = orth_with(panel, gram_left)
         partial_wide = jnp.dot(left, target, precision=HIGH)

time: 837 us -> 742 us (0.89)
  waiting for transfers between devices: 422 us -> 327 us
    psum x2 -> x0, waiting for transfers between devices: 130 us -> none  [per_device(): panel = lax.psum(partial_left, 'gal')]
    ppermute x0 -> x6, waiting for transfers between devices: none -> 32.9 us  [add_in_pairs(): result = result + lax.ppermute(result, name, pairs)]
  transfers between devices with their start and end apart: 4 -> 8, of which waited for: 4 -> 8; matrix products, arithmetic and copies ran while one was open for 0% -> 0% of each run, Pallas kernels for 0% -> 0%
where the time goes in v1:
time: 742 us
  waiting for transfers between devices  327 us (44%)
  blocking collectives  310 us (42%)
  other arithmetic  48.5 us (7%)
  matrix products  35.2 us (5%)
  between operations  14.3 us (2%)
    psum x2, waiting for transfers between devices, per_device(): wide = lax.psum(partial_wide, 'pix')  295 us
    psum x2, blocking collectives, per_device(): gram_left = lax.psum(gram_of(panel), 'pix')  263 us
    psum x2, blocking collectives, per_device(): gram_right = lax.psum(gram_of(wide), 'gal')  47.4 us
    ppermute x6, waiting for transfers between devices, add_in_pairs(): result = result + lax.ppermute(result, name, pairs)  32.9 us
    another operation x12, other arithmetic, orth_with(): factor = jnp.linalg.cholesky(gram)  26.1 us
    another operation x8, other arithmetic, orth_with(): return jax.scipy.linalg.solve_triangular(factor, panel, lower=True)  22.2 us
  transfers between devices with their start and end apart: 8, of which 8 were waited for; matrix products, arithmetic and copies ran while one was open for 0% of the time, Pallas kernels for 0%

profile of v1, /device:TPU:2, one launch (start us, length us, event | category | flops | bytes accessed | tf_op | source)
XLA Modules:
  0.0 742.1 jit_solution(4524972640222490992)
XLA Ops:
  7.2 0.8 copy-done
  8.1 5.2 convolution_bitcast_fusion
  13.3 0.1 collective-permute-start
  13.4 1.5 collective-permute-done
  14.9 1.7 collective-permute-start.1
  16.6 6.8 collective-permute-done.1
  23.4 3.3 collective-permute-start.2
  26.7 5.8 collective-permute-done.2
  32.5 0.4 fusion.21
  32.9 133.6 %psum.42 = f32[64,64]{0,1:T(8,128)S(1)} all-reduce(f32[64,64]{0,1:T(8,128)S(1)} %fusion.21), channel_id=1, replica_groups=mesh['gal'=8,'pix'=32] {'pix'}, use_global_device_ids=true, to_apply=%region_0.0 | all-reduce | flops 4096 | bytes 32768 | tf_op jit(solution)/shard_map/psum | solution.py:40
  166.6 5.8 cholesky.74
  172.5 0.6 compare_reduce_fusion.3
  173.1 0.7 fusion
  173.8 4.9 custom-call.10
  178.7 0.4 fusion.13
  179.1 4.4 fusion.20
  183.6 148.5 %all-reduce.3.cloned.1.call-done = f32[64,512]{1,0:T(8,128)} async-done(((f32[64,512]{1,0:T(8,128)}), f32[64,512]{1,0:T(8,128)}) %all-reduce.3.cloned.1.call-update) | async-done | bytes 131088 | tf_op jit(solution)/shard_map/psum | solution.py:43
  332.1 1.2 fusion.22
  333.4 23.8 %psum.44 = f32[64,64]{0,1:T(8,128)S(1)} all-reduce(f32[64,64]{0,1:T(8,128)S(1)} %fusion.22), channel_id=1, replica_groups=mesh['gal'=8,'pix'=32] {'gal'}, use_global_device_ids=true, to_apply=%region_4.7 | all-reduce | flops 4096 | bytes 32768 | tf_op jit(solution)/shard_map/psum | solution.py:47
  357.3 5.8 cholesky.85
  363.1 0.6 compare_reduce_fusion.2
  363.8 0.7 fusion.1
  364.4 4.9 custom-call.11
  369.4 6.1 subtract_add_fusion
  375.5 0.3 fusion.10
  375.8 2.1 fusion.23
  378.1 1.5 collective-permute-done.3
  379.6 0.1 collective-permute-start.4
  379.7 8.3 %collective-permute-done.4 = f32[64,1024]{1,0:T(8,128)S(1)} collective-permute-done((f32[64,1024]{1,0:T(8,128)S(1)}, f32[64,1024]{1,0:T(8,128)S(1)}, u32[]{:S(2)}, u32[]{:S(2)}) %collective-permute-start.4) | collective-permute-done | bytes 262176 | tf_op jit(solution)/shard_map/ppermute | solution.py:16
  388.1 0.1 collective-permute-start.5
  388.2 9.0 %collective-permute-done.5 = f32[64,1024]{1,0:T(8,128)S(1)} collective-permute-done((f32[64,1024]{1,0:T(8,128)S(1)}, f32[64,1024]{1,0:T(8,128)S(1)}, u32[]{:S(2)}, u32[]{:S(2)}) %collective-permute-start.5) | collective-permute-done | bytes 262176 | tf_op jit(solution)/shard_map/ppermute | solution.py:16
  397.2 0.4 fusion.24
  397.6 129.1 %psum.45 = f32[64,64]{0,1:T(8,128)S(1)} all-reduce(f32[64,64]{0,1:T(8,128)S(1)} %fusion.24), channel_id=1, replica_groups=mesh['gal'=8,'pix'=32] {'pix'}, use_global_device_ids=true, to_apply=%region_5.0 | all-reduce | flops 4096 | bytes 32768 | tf_op jit(solution)/shard_map/psum | solution.py:40
  526.8 5.8 cholesky.96
  532.6 0.6 compare_reduce_fusion.1
  533.3 0.7 fusion.2
  533.9 4.9 custom-call.12
  538.8 0.4 fusion.7
  539.3 3.7 fusion.25
  543.0 146.0 %all-reduce.5.cloned.1.call-done = f32[64,512]{1,0:T(8,128)} async-done(((f32[64,512]{1,0:T(8,128)}), f32[64,512]{1,0:T(8,128)}) %all-reduce.5.cloned.1.call-update) | async-done | bytes 131088 | tf_op jit(solution)/shard_map/psum | solution.py:43
  689.0 1.2 fusion.26
  690.3 23.6 %psum.47 = f32[64,64]{0,1:T(8,128)S(1)} all-reduce(f32[64,64]{0,1:T(8,128)S(1)} %fusion.26), channel_id=1, replica_groups=mesh['gal'=8,'pix'=32] {'gal'}, use_global_device_ids=true, to_apply=%region_7.11 | all-reduce | flops 4096 | bytes 32768 | tf_op jit(solution)/shard_map/psum | solution.py:47
  714.0 5.8 cholesky.107
  719.8 0.6 compare_reduce_fusion
  720.5 0.7 fusion.3
  721.1 4.9 custom-call.13
  726.1 8.2 %multiply_add_fusion = (f32[1024,512]{1,0:T(8,128)}, f32[1024,512]{1,0:T(8,128)}) fusion(f32[1024,512]{1,0:T(8,128)S(1)} %copy-done.1, f32[1024,512]{1,0:T(8,128)} %get-tuple-element.10, f32[1024,512]{1,0:T(8,128)} %param.9, f32[64,1024]{1,0:T(8,128)S(1)} %fusion.7, f32[64,512]{1,0:T(8,128)} %all-reduce.5.cloned.1.call-done), kind=kOutput, calls=%fused_computation | convolution fusion | flops 413663232 | bytes 10878976 | tf_op jit(solution)/shard_map/dot_general | solution.py:44
  734.3 1.0 fusion.4
  (34 shorter events, 0.9 us)
Async XLA Ops:
  7.2 0.9 copy-start
  7.2 325.0 %all-reduce.3.cloned.1.call-start = ((), (), s32[]{:S(2)}) async-start(), calls=%async_computation | async-start | bytes 262144 | tf_op jit(solution)/shard_map/psum | solution.py:43
  13.3 165.8 %copy-start.1 = (f32[1024,512]{1,0:T(8,128)S(1)}, f32[1024,512]{1,0:T(8,128)}, u32[]{:S(2)}) copy-start(f32[1024,512]{1,0:T(8,128)} %param.11) | copy-start | bytes 6291460
  13.3 1.6 collective-permute-start
  14.9 8.4 %collective-permute-start.1 = (f32[64,1024]{1,0:T(8,128)S(1)}, f32[64,1024]{1,0:T(8,128)S(1)}, u32[]{:S(2)}, u32[]{:S(2)}) collective-permute-start(f32[64,1024]{1,0:T(8,128)S(1)} %add.62), channel_id=1, source_target_pairs={{0,64},{32,96},{64,0},{96,32},{128,192},{160,224},{192,128},{224,1... | collective-permute-start | bytes 786440 | tf_op jit(solution)/shard_map/ppermute | solution.py:16
  23.4 9.1 %collective-permute-start.2 = (f32[64,1024]{1,0:T(8,128)S(1)}, f32[64,1024]{1,0:T(8,128)S(1)}, u32[]{:S(2)}, u32[]{:S(2)}) collective-permute-start(f32[64,1024]{1,0:T(8,128)S(1)} %add.63), channel_id=1, source_target_pairs={{0,128},{32,160},{64,192},{96,224},{128,0},{160,32},{192,64},{224,... | collective-permute-start | bytes 786440 | tf_op jit(solution)/shard_map/ppermute | solution.py:16
  183.6 505.5 %all-reduce.5.cloned.1.call-start = ((), (), s32[]{:S(2)}) async-start(), calls=%async_computation.1 | async-start | bytes 262144 | tf_op jit(solution)/shard_map/psum | solution.py:43
  369.3 6.2 copy-start.4
  375.5 12.6 %copy-start.2 = (f32[1024,512]{1,0:T(8,128)}, f32[1024,512]{1,0:T(8,128)S(1)}, u32[]{:S(2)}) copy-start(f32[1024,512]{1,0:T(8,128)S(1)} %get-tuple-element.9) | copy-start | bytes 6291460
  378.0 1.6 collective-permute-start.3
  379.6 8.4 %collective-permute-start.4 = (f32[64,1024]{1,0:T(8,128)S(1)}, f32[64,1024]{1,0:T(8,128)S(1)}, u32[]{:S(2)}, u32[]{:S(2)}) collective-permute-start(f32[64,1024]{1,0:T(8,128)S(1)} %add.68), channel_id=1, source_target_pairs={{0,64},{32,96},{64,0},{96,32},{128,192},{160,224},{192,128},{224,1... | collective-permute-start | bytes 786440 | tf_op jit(solution)/shard_map/ppermute | solution.py:16
  388.1 9.1 %collective-permute-start.5 = (f32[64,1024]{1,0:T(8,128)S(1)}, f32[64,1024]{1,0:T(8,128)S(1)}, u32[]{:S(2)}, u32[]{:S(2)}) collective-permute-start(f32[64,1024]{1,0:T(8,128)S(1)} %add.69), channel_id=1, source_target_pairs={{0,128},{32,160},{64,192},{96,224},{128,0},{160,32},{192,64},{224,... | collective-permute-start | bytes 786440 | tf_op jit(solution)/shard_map/ppermute | solution.py:16
  539.3 195.0 %copy-start.3 = (f32[64,1024]{1,0:T(8,128)}, f32[64,1024]{1,0:T(8,128)S(1)}, u32[]{:S(2)}) copy-start(f32[64,1024]{1,0:T(8,128)S(1)} %fusion.7) | copy-start | bytes 786436
  726.0 8.3 %copy-start.5 = (f32[64,512]{1,0:T(8,128)S(1)}, f32[64,512]{1,0:T(8,128)}, u32[]{:S(2)}) copy-start(f32[64,512]{1,0:T(8,128)} %all-reduce.5.cloned.1.call-done) | copy-start | bytes 393220
Sparse Core Ops, SparseCore 0:
  183.7 148.4 all-reduce.2
  543.2 145.8 all-reduce.4
